TPU v7x, 32 devices: a whole 2x2x4 slice. The times are simulated.
32 devices in a mesh: domain: 2 (over x), fsdp: 16 (over z, y, core).
Axes of the slice: x: 2, y: 2, z: 4, core: 2. Of those that a mesh axis runs over, the one named last changes fastest.
Arguments:
- gradients: bfloat16 [2, 4, 4096, 512], P('domain', None, 'fsdp')
- row_counts: int32 [4], replicated, may hold values from 2048 to 4096, as said below
- domain_ids: int32 [2], replicated, may hold values from 0 to 7
- domain_weights: float32 [8], replicated, may hold values from 0.2 to 2
Outputs:
- updates: float32 [4, 4096, 512], P('domain', 'fsdp')
- new_weights: float32 [8], replicated
Inputs may be any that keep to these rules, and one draw needn't show every extreme that they name: `row_counts`: each matrix has 4096 or 2048 rows, and both counts occur.
All inputs are finite; a program needn't handle non-finite values.
Results may differ from a plain program's by a relative error of at most 0.0071.
Values may be sent and summed in bfloat16 or wider, within the bound.
No kernel may reach another device: no remote copies, remote signals or barrier semaphores. Data moves between devices by JAX's collectives and lax.ppermute only.
A program may use at most 64 MiB of HBM per device.

v0:
```python
import math
import jax
import jax.numpy as jnp
from jax import lax
from jax.sharding import PartitionSpec as P

NS_ITERS = 3
OWNERS = 8
COEF_A = 3.4445
COEF_B = -4.775
COEF_C = 2.0315
MUON_SCALE = 0.2
ETA = 4.0


def partner(shard, axis, stride):
    return lax.ppermute(shard, axis, [(i, i ^ 1 << stride) for i in range(lax.axis_size(axis))])


def group_mixing(domain_ids, domain_weights, kind_count):
    weight_share = domain_weights / jnp.sum(domain_weights)
    onehot = (domain_ids[:, None] == jnp.arange(kind_count, dtype=jnp.int32)[None, :]).astype(
        jnp.float32
    )
    counts = jnp.sum(onehot, axis=0)
    per_member = weight_share / jnp.maximum(counts, 1.0)
    group_mix = jnp.sum(onehot * per_member[None, :], axis=1)
    return (weight_share, onehot, counts, group_mix)


def summed_gram(iterate):
    gram_total = lax.dot_general(
        iterate, iterate, (((0,), (0,)), ((), ())), preferred_element_type=jnp.float32
    )
    for bit_pos in range(OWNERS.bit_length() - 1):
        gram_total = gram_total + partner(gram_total, "fsdp", bit_pos)
    return gram_total


def newton_steps(iterate):
    for repeat in range(NS_ITERS):
        gram_full = lax.optimization_barrier(summed_gram(iterate).astype(jnp.bfloat16))
        square = jnp.dot(gram_full, gram_full, preferred_element_type=jnp.float32)
        poly_term = (COEF_B * gram_full.astype(jnp.float32) + COEF_C * square).astype(jnp.bfloat16)
        iterate = lax.optimization_barrier(
            (
                COEF_A * iterate.astype(jnp.float32)
                + jnp.dot(iterate, poly_term, preferred_element_type=jnp.float32)
            ).astype(jnp.bfloat16)
        )
    return iterate


def share_scores(aligned, squares, norm_slots):
    return lax.psum((aligned, squares, norm_slots), ("domain", "fsdp"))


def body(gradients, row_counts, domain_ids, domain_weights):
    groups = lax.axis_size("domain")
    shards = lax.axis_size("fsdp")
    matrices = row_counts.shape[0]
    rows_src = gradients.shape[2]
    columns = gradients.shape[3]
    per_domain = matrices // groups
    sub_rows = rows_src // OWNERS
    own_rows = shards * sub_rows
    full_rows = rows_src * shards
    domain_pos = lax.axis_index("domain")
    shard_pos = lax.axis_index("fsdp")
    weight_share, onehot, counts, group_mix = group_mixing(
        domain_ids, domain_weights, domain_weights.shape[0]
    )
    blocks = lax.all_to_all(
        gradients.reshape(1, groups, per_domain, rows_src, columns),
        "domain",
        split_axis=1,
        concat_axis=0,
        tiled=True,
    )
    blocks = blocks.reshape(groups, per_domain, rows_src, columns)
    global_rows = shard_pos * rows_src + jnp.arange(rows_src, dtype=jnp.int32)
    limits = lax.dynamic_slice_in_dim(row_counts, domain_pos * per_domain, per_domain, 0)
    row_mask = (global_rows[None, :] < limits[:, None])[None, :, :, None]
    masked = jnp.where(row_mask, blocks.astype(jnp.float32), jnp.zeros((), jnp.float32))
    combined = jnp.sum(group_mix[:, None, None, None] * masked, axis=0)
    aligned = jnp.sum(masked * combined[None], axis=(1, 2, 3))
    squares = jnp.sum(masked * masked, axis=(1, 2, 3))
    block_squares = jnp.sum(combined * combined, axis=(1, 2))
    norm_slots = lax.dynamic_update_slice_in_dim(
        jnp.zeros((matrices,), jnp.float32), block_squares, domain_pos * per_domain, 0
    )
    aligned, squares, norm_slots = share_scores(aligned, squares, norm_slots)
    frob_norm = (
        jnp.sqrt(lax.dynamic_slice_in_dim(norm_slots, domain_pos * per_domain, per_domain, 0))
        + 1e-07
    )
    scaled = (combined / frob_norm[:, None, None]).astype(jnp.bfloat16)
    scaled = scaled.reshape(shards, 1, sub_rows, columns)
    start_rows = lax.all_to_all(scaled, "fsdp", split_axis=0, concat_axis=1, tiled=True)
    start_rows = lax.optimization_barrier(start_rows.reshape(own_rows, columns))
    finished = newton_steps(start_rows)
    returned = lax.all_to_all(
        finished.reshape(1, shards, sub_rows, columns),
        "fsdp",
        split_axis=1,
        concat_axis=0,
        tiled=True,
    )
    returned = returned.reshape(per_domain, rows_src, columns)
    updates = returned.astype(jnp.float32) * (MUON_SCALE * math.sqrt(full_rows))
    total_sq = jnp.sum(norm_slots)
    cosine = aligned / (jnp.sqrt(squares) * jnp.sqrt(total_sq) + 1e-06)
    score = jnp.sum(onehot * cosine[:, None], axis=0) / jnp.maximum(counts, 1.0)
    raised = weight_share * jnp.exp(ETA * score)
    return (updates, raised / jnp.sum(raised))


def solution(mesh):
    placed = (P("domain", None, "fsdp", None), P(), P(), P())
    return jax.shard_map(
        body,
        mesh=mesh,
        in_specs=placed,
        out_specs=(P("domain", "fsdp", None), P()),
        check_vma=False,
    )
```

profile of v0, /device:TPU:0, one launch (start us, length us, event | category | flops | bytes accessed | tf_op | source)
XLA Modules:
  0.0 265.7 jit_solution(6877497156156330844)
XLA Ops:
  0.7 4.4 %all-to-all-start = ((bf16[1,2,2,256,512]{4,3,2,0,1:T(8,128)(2,1)}), bf16[1,2,2,256,512]{4,3,2,0,1:T(8,128)(2,1)S(1)}, u32[]{:S(2)}, u32[]{:S(2)}) async-start(bf16[1,2,2,256,512]{4,3,2,0,1:T(8,128)(2,1)} %bitcast.31), calls=%async_computation | async-start | bytes 2097152 | tf_op jit(solution)/shard_map/all_to_all | solution.py:73
  5.1 0.6 reduce_sum.92
  5.8 0.7 multiply_divide_fusion
  6.7 12.7 %all-to-all-done = bf16[1,2,2,256,512]{4,3,2,0,1:T(8,128)(2,1)S(1)} async-done(((bf16[1,2,2,256,512]{4,3,2,0,1:T(8,128)(2,1)}), bf16[1,2,2,256,512]{4,3,2,0,1:T(8,128)(2,1)S(1)}, u32[]{:S(2)}, u32[]{:S(2)}) %all-to-all-start) | async-done | bytes 1048608 | tf_op jit(solution)/shard_map/all_to_all | solution.py:73
  20.2 0.7 fusion.5
  20.9 39.8 %all-reduce = (f32[4]{0:T(128)S(1)}, f32[2]{0:T(128)S(1)}, f32[2]{0:T(128)S(1)}) all-reduce(f32[4]{0:T(128)S(1)} %dynamic_update_slice.3, f32[2]{0:T(128)S(1)} %get-tuple-element.3, f32[2]{0:T(128)S(1)} %get-tuple-element.2), channel_id=1, replica_groups=mesh['domain'=2,'fsdp'=16] {'domain','fsdp'}, use_global_device_ids=true, to_apply=%region_5.6 | all-reduce | flops 8 | bytes 64 | tf_op jit(solution)/shard_map/psum | solution.py:55
  60.7 0.6 reduce_sum.100
  62.4 19.5 %all_to_all.12 = bf16[16,1,32,512]{3,2,1,0:T(8,128)(2,1)S(1)} all-to-all(bf16[16,1,32,512]{3,2,1,0:T(8,128)(2,1)S(1)} %divide_convert_fusion), channel_id=1, replica_groups=mesh['domain'=2,'fsdp'=16] {'fsdp'}, dimensions={0} | all-to-all | bytes 1048576 | tf_op jit(solution)/shard_map/all_to_all | solution.py:99
  81.9 0.5 fusion.22
  82.6 2.5 collective-permute-done
  85.3 1.1 collective-permute-start.1
  86.4 24.2 %collective-permute-done.1 = f32[512,512]{1,0:T(8,128)S(1)} collective-permute-done((f32[512,512]{1,0:T(8,128)S(1)}, f32[512,512]{1,0:T(8,128)S(1)}, u32[]{:S(2)}, u32[]{:S(2)}) %collective-permute-start.1) | collective-permute-done | bytes 1048608 | tf_op jit(solution)/shard_map/ppermute | solution.py:17
  110.8 1.8 collective-permute-start.2
  112.6 22.8 %collective-permute-done.2 = f32[512,512]{1,0:T(8,128)S(1)} collective-permute-done((f32[512,512]{1,0:T(8,128)S(1)}, f32[512,512]{1,0:T(8,128)S(1)}, u32[]{:S(2)}, u32[]{:S(2)}) %collective-permute-start.2) | collective-permute-done | bytes 1048608 | tf_op jit(solution)/shard_map/ppermute | solution.py:17
  135.7 0.8 fusion.6
  137.0 2.6 collective-permute-done.3
  139.9 1.3 collective-permute-start.4
  141.2 23.9 %collective-permute-done.4 = f32[512,512]{1,0:T(8,128)S(1)} collective-permute-done((f32[512,512]{1,0:T(8,128)S(1)}, f32[512,512]{1,0:T(8,128)S(1)}, u32[]{:S(2)}, u32[]{:S(2)}) %collective-permute-start.4) | collective-permute-done | bytes 1048608 | tf_op jit(solution)/shard_map/ppermute | solution.py:17
  165.4 1.8 collective-permute-start.5
  167.2 22.6 %collective-permute-done.5 = f32[512,512]{1,0:T(8,128)S(1)} collective-permute-done((f32[512,512]{1,0:T(8,128)S(1)}, f32[512,512]{1,0:T(8,128)S(1)}, u32[]{:S(2)}, u32[]{:S(2)}) %collective-permute-start.5) | collective-permute-done | bytes 1048608 | tf_op jit(solution)/shard_map/ppermute | solution.py:17
  190.0 0.8 fusion.7
  191.4 2.6 collective-permute-done.6
  194.2 1.3 collective-permute-start.7
  195.6 23.9 %collective-permute-done.7 = f32[512,512]{1,0:T(8,128)S(1)} collective-permute-done((f32[512,512]{1,0:T(8,128)S(1)}, f32[512,512]{1,0:T(8,128)S(1)}, u32[]{:S(2)}, u32[]{:S(2)}) %collective-permute-start.7) | collective-permute-done | bytes 1048608 | tf_op jit(solution)/shard_map/ppermute | solution.py:17
  219.7 1.8 collective-permute-start.8
  221.5 22.6 %collective-permute-done.8 = f32[512,512]{1,0:T(8,128)S(1)} collective-permute-done((f32[512,512]{1,0:T(8,128)S(1)}, f32[512,512]{1,0:T(8,128)S(1)}, u32[]{:S(2)}, u32[]{:S(2)}) %collective-permute-start.8) | collective-permute-done | bytes 1048608 | tf_op jit(solution)/shard_map/ppermute | solution.py:17
  244.4 1.6 fusion.8
  245.9 4.4 %all-to-all-start.2 = ((bf16[1,16,32,512]{3,2,0,1:T(8,128)(2,1)}), bf16[1,16,32,512]{3,2,0,1:T(8,128)(2,1)S(1)}, u32[]{:S(2)}, u32[]{:S(2)}) async-start(bf16[1,16,32,512]{3,2,0,1:T(8,128)(2,1)} %bitcast.5), calls=%async_computation.2 | async-start | bytes 1048576 | tf_op jit(solution)/shard_map/all_to_all | solution.py:102
  250.4 1.3 fusion.21
  251.8 1.2 broadcast_divide_fusion
  253.0 11.6 %all-to-all-done.2 = bf16[1,16,32,512]{3,2,0,1:T(8,128)(2,1)S(1)} async-done(((bf16[1,16,32,512]{3,2,0,1:T(8,128)(2,1)}), bf16[1,16,32,512]{3,2,0,1:T(8,128)(2,1)S(1)}, u32[]{:S(2)}, u32[]{:S(2)}) %all-to-all-start.2) | async-done | bytes 524320 | tf_op jit(solution)/shard_map/all_to_all | solution.py:102
  264.6 1.1 convert_multiply_fusion
  (34 shorter events, 5.0 us)
Async XLA Ops:
  0.6 4.4 %copy-start.2 = (s32[2]{0:T(128)S(1)}, s32[2]{0:T(128)}, u32[]{:S(2)}) copy-start(s32[2]{0:T(128)} %param.6) | copy-start | bytes 28
  0.6 4.5 %copy-start = (f32[8]{0:T(128)S(1)}, f32[8]{0:T(128)}, u32[]{:S(2)}) copy-start(f32[8]{0:T(128)} %param.7) | copy-start | bytes 100
  0.7 5.1 %copy-start.1 = (s32[4]{0:T(128)S(1)}, s32[4]{0:T(128)}, u32[]{:S(2)}) copy-start(s32[4]{0:T(128)} %param.5) | copy-start | bytes 52
  0.7 18.8 %all-to-all-start = ((bf16[1,2,2,256,512]{4,3,2,0,1:T(8,128)(2,1)}), bf16[1,2,2,256,512]{4,3,2,0,1:T(8,128)(2,1)S(1)}, u32[]{:S(2)}, u32[]{:S(2)}) async-start(bf16[1,2,2,256,512]{4,3,2,0,1:T(8,128)(2,1)} %bitcast.31), calls=%async_computation | async-start | bytes 2097152 | tf_op jit(solution)/shard_map/all_to_all | solution.py:73
  82.4 2.7 %collective-permute-start = (f32[512,512]{1,0:T(8,128)S(1)}, f32[512,512]{1,0:T(8,128)S(1)}, u32[]{:S(2)}, u32[]{:S(2)}) collective-permute-start(f32[512,512]{1,0:T(8,128)S(1)} %fusion.22), channel_id=1, source_target_pairs={{0,1},{1,0},{2,3},{3,2},{4,5},{5,4},{6,7},{7,6},{8,9},{9,8},{10,11... | collective-permute-start | bytes 3145736 | tf_op jit(solution)/shard_map/ppermute | solution.py:17
  85.3 25.3 %collective-permute-start.1 = (f32[512,512]{1,0:T(8,128)S(1)}, f32[512,512]{1,0:T(8,128)S(1)}, u32[]{:S(2)}, u32[]{:S(2)}) collective-permute-start(f32[512,512]{1,0:T(8,128)S(1)} %add.76), channel_id=1, source_target_pairs={{0,2},{1,3},{2,0},{3,1},{4,6},{5,7},{6,4},{7,5},{8,10},{9,11},{10,... | collective-permute-start | bytes 3145736 | tf_op jit(solution)/shard_map/ppermute | solution.py:17
  110.8 24.7 %collective-permute-start.2 = (f32[512,512]{1,0:T(8,128)S(1)}, f32[512,512]{1,0:T(8,128)S(1)}, u32[]{:S(2)}, u32[]{:S(2)}) collective-permute-start(f32[512,512]{1,0:T(8,128)S(1)} %add.77), channel_id=1, source_target_pairs={{0,4},{1,5},{2,6},{3,7},{4,0},{5,1},{6,2},{7,3},{8,12},{9,13},{10,... | collective-permute-start | bytes 3145736 | tf_op jit(solution)/shard_map/ppermute | solution.py:17
  137.0 2.7 %collective-permute-start.3 = (f32[512,512]{1,0:T(8,128)S(1)}, f32[512,512]{1,0:T(8,128)S(1)}, u32[]{:S(2)}, u32[]{:S(2)}) collective-permute-start(f32[512,512]{1,0:T(8,128)S(1)} %fusion.23), channel_id=1, source_target_pairs={{0,1},{1,0},{2,3},{3,2},{4,5},{5,4},{6,7},{7,6},{8,9},{9,8},{10,11... | collective-permute-start | bytes 3145736 | tf_op jit(solution)/shard_map/ppermute | solution.py:17
  139.9 25.3 %collective-permute-start.4 = (f32[512,512]{1,0:T(8,128)S(1)}, f32[512,512]{1,0:T(8,128)S(1)}, u32[]{:S(2)}, u32[]{:S(2)}) collective-permute-start(f32[512,512]{1,0:T(8,128)S(1)} %add.81), channel_id=1, source_target_pairs={{0,2},{1,3},{2,0},{3,1},{4,6},{5,7},{6,4},{7,5},{8,10},{9,11},{10,... | collective-permute-start | bytes 3145736 | tf_op jit(solution)/shard_map/ppermute | solution.py:17
  165.4 24.4 %collective-permute-start.5 = (f32[512,512]{1,0:T(8,128)S(1)}, f32[512,512]{1,0:T(8,128)S(1)}, u32[]{:S(2)}, u32[]{:S(2)}) collective-permute-start(f32[512,512]{1,0:T(8,128)S(1)} %add.82), channel_id=1, source_target_pairs={{0,4},{1,5},{2,6},{3,7},{4,0},{5,1},{6,2},{7,3},{8,12},{9,13},{10,... | collective-permute-start | bytes 3145736 | tf_op jit(solution)/shard_map/ppermute | solution.py:17
  191.3 2.7 %collective-permute-start.6 = (f32[512,512]{1,0:T(8,128)S(1)}, f32[512,512]{1,0:T(8,128)S(1)}, u32[]{:S(2)}, u32[]{:S(2)}) collective-permute-start(f32[512,512]{1,0:T(8,128)S(1)} %fusion.24), channel_id=1, source_target_pairs={{0,1},{1,0},{2,3},{3,2},{4,5},{5,4},{6,7},{7,6},{8,9},{9,8},{10,11... | collective-permute-start | bytes 3145736 | tf_op jit(solution)/shard_map/ppermute | solution.py:17
  194.2 25.3 %collective-permute-start.7 = (f32[512,512]{1,0:T(8,128)S(1)}, f32[512,512]{1,0:T(8,128)S(1)}, u32[]{:S(2)}, u32[]{:S(2)}) collective-permute-start(f32[512,512]{1,0:T(8,128)S(1)} %add.86), channel_id=1, source_target_pairs={{0,2},{1,3},{2,0},{3,1},{4,6},{5,7},{6,4},{7,5},{8,10},{9,11},{10,... | collective-permute-start | bytes 3145736 | tf_op jit(solution)/shard_map/ppermute | solution.py:17
  219.7 24.4 %collective-permute-start.8 = (f32[512,512]{1,0:T(8,128)S(1)}, f32[512,512]{1,0:T(8,128)S(1)}, u32[]{:S(2)}, u32[]{:S(2)}) collective-permute-start(f32[512,512]{1,0:T(8,128)S(1)} %add.87), channel_id=1, source_target_pairs={{0,4},{1,5},{2,6},{3,7},{4,0},{5,1},{6,2},{7,3},{8,12},{9,13},{10,... | collective-permute-start | bytes 3145736 | tf_op jit(solution)/shard_map/ppermute | solution.py:17
  245.9 18.7 %all-to-all-start.2 = ((bf16[1,16,32,512]{3,2,0,1:T(8,128)(2,1)}), bf16[1,16,32,512]{3,2,0,1:T(8,128)(2,1)S(1)}, u32[]{:S(2)}, u32[]{:S(2)}) async-start(bf16[1,16,32,512]{3,2,0,1:T(8,128)(2,1)} %bitcast.5), calls=%async_computation.2 | async-start | bytes 1048576 | tf_op jit(solution)/shard_map/all_to_all | solution.py:102
where the time goes:
time: 266 us
  waiting for transfers between devices  172 us (65%)
  blocking collectives  59.3 us (22%)
  starting transfers between devices  18.3 us (7%)
  other arithmetic  9.43 us (4%)
  matrix products  4.55 us (2%)
    ppermute x9, waiting for transfers between devices, partner(): lax.ppermute(shard, axis, [(i, i ^ 1 << stride) for i in range(lax.axis_s...  148 us
    psum x1, blocking collectives, share_scores(): return lax.psum((aligned, squares, norm_slots), ('domain', 'fsdp'))  39.8 us
    all_to_all x1, blocking collectives, body(): lax.all_to_all(scaled, 'fsdp', split_axis=0, concat_axis=1, tiled=True)  19.5 us
    all_to_all x1, waiting for transfers between devices, body(): lax.all_to_all(gradients.reshape(1, groups, per_domain, rows_src, columns...  12.7 us
    all_to_all x1, waiting for transfers between devices, body(): lax.all_to_all(finished.reshape(1, shards, sub_rows, columns), 'fsdp', sp...  11.6 us
    ppermute x9, starting transfers between devices, partner(): lax.ppermute(shard, axis, [(i, i ^ 1 << stride) for i in range(lax.axis_s...  9.5 us
  transfers between devices with their start and end apart: 11, of which 11 were waited for; matrix products, arithmetic and copies ran while one was open for 2% of the time, Pallas kernels for 0%

commit v1 on v0

--- a/solution.py
+++ b/solution.py
@@ -11,6 +11,11 @@
 COEF_C = 2.0315
 MUON_SCALE = 0.2
 ETA = 4.0
+
+
+def by_each_axis(array, inner_axis, outer_axis):
+    half = lax.psum(array, inner_axis)
+    return lax.psum(half, outer_axis)
 
 
 def partner(shard, axis, stride):
@@ -52,7 +57,7 @@
 
 
 def share_scores(aligned, squares, norm_slots):
-    return lax.psum((aligned, squares, norm_slots), ("domain", "fsdp"))
+    return by_each_axis((aligned, squares, norm_slots), "fsdp", "domain")
 
 
 def body(gradients, row_counts, domain_ids, domain_weights):

time: 266 us -> 262 us (0.985)
  blocking collectives: 59.3 us -> 54.7 us
    psum x1 -> x2, blocking collectives: 39.8 us -> 37.8 us  [the longest x1 32.9 us: by_each_axis(): half = lax.psum(array, inner_axis)]
where the time goes in v1:
time: 262 us; the launch traced here: 261 us
  waiting for transfers between devices  172 us (66%)
  blocking collectives  54.7 us (21%)
  starting transfers between devices  18.1 us (7%)
  other arithmetic  9.43 us (4%)
  matrix products  4.54 us (2%)
    ppermute x9, waiting for transfers between devices, partner(): lax.ppermute(shard, axis, [(i, i ^ 1 << stride) for i in range(lax.axis_s...  148 us
    psum x1, blocking collectives, by_each_axis(): half = lax.psum(array, inner_axis)  32.9 us
    all_to_all x1, blocking collectives, body(): lax.all_to_all(scaled, 'fsdp', split_axis=0, concat_axis=1, tiled=True)  16.9 us
    all_to_all x1, waiting for transfers between devices, body(): lax.all_to_all(gradients.reshape(1, groups, per_domain, rows_src, columns...  12.7 us
    all_to_all x1, waiting for transfers between devices, body(): lax.all_to_all(finished.reshape(1, shards, sub_rows, columns), 'fsdp', sp...  11.6 us
    ppermute x9, starting transfers between devices, partner(): lax.ppermute(shard, axis, [(i, i ^ 1 << stride) for i in range(lax.axis_s...  9.42 us
  transfers between devices with their start and end apart: 11, of which 11 were waited for; matrix products, arithmetic and copies ran while one was open for 2% of the time, Pallas kernels for 0%

profile of v1, /device:TPU:0, one launch (start us, length us, event | category | flops | bytes accessed | tf_op | source)
XLA Modules:
  0.0 261.1 jit_solution(4482531152342902894)
XLA Ops:
  0.7 4.4 %all-to-all-start = ((bf16[1,2,2,256,512]{4,3,2,0,1:T(8,128)(2,1)}), bf16[1,2,2,256,512]{4,3,2,0,1:T(8,128)(2,1)S(1)}, u32[]{:S(2)}, u32[]{:S(2)}) async-start(bf16[1,2,2,256,512]{4,3,2,0,1:T(8,128)(2,1)} %bitcast.31), calls=%async_computation | async-start | bytes 2097152 | tf_op jit(solution)/shard_map/all_to_all | solution.py:78
  5.1 0.6 reduce_sum.92
  5.8 0.7 multiply_divide_fusion
  6.7 12.7 %all-to-all-done = bf16[1,2,2,256,512]{4,3,2,0,1:T(8,128)(2,1)S(1)} async-done(((bf16[1,2,2,256,512]{4,3,2,0,1:T(8,128)(2,1)}), bf16[1,2,2,256,512]{4,3,2,0,1:T(8,128)(2,1)S(1)}, u32[]{:S(2)}, u32[]{:S(2)}) %all-to-all-start) | async-done | bytes 1048608 | tf_op jit(solution)/shard_map/all_to_all | solution.py:78
  20.2 0.7 fusion.5
  20.9 32.9 %all-reduce = (f32[4]{0:T(128)S(1)}, f32[2]{0:T(128)S(1)}, f32[2]{0:T(128)S(1)}) all-reduce(f32[4]{0:T(128)S(1)} %dynamic_update_slice.3, f32[2]{0:T(128)S(1)} %get-tuple-element.3, f32[2]{0:T(128)S(1)} %get-tuple-element.2), channel_id=1, replica_groups=mesh['domain'=2,'fsdp'=16] {'fsdp'}, use_global_device_ids=true, to_apply=%region_5.6 | all-reduce | flops 8 | bytes 64 | tf_op jit(solution)/shard_map/psum | solution.py:17
  53.8 4.9 %all-reduce.1 = (f32[4]{0:T(128)S(1)}, f32[2]{0:T(128)S(1)}, f32[2]{0:T(128)S(1)}) all-reduce(f32[4]{0:T(128)S(1)} %get-tuple-element.4, f32[2]{0:T(128)S(1)} %get-tuple-element.5, f32[2]{0:T(128)S(1)} %get-tuple-element.6), channel_id=1, replica_groups=mesh['domain'=2,'fsdp'=16] {'domain'}, use_global_device_ids=true, to_apply=%region_6.7 | all-reduce | flops 8 | bytes 64 | tf_op jit(solution)/shard_map/psum | solution.py:18
  58.7 0.6 reduce_sum.100
  60.4 16.9 %all_to_all.12 = bf16[16,1,32,512]{3,2,1,0:T(8,128)(2,1)S(1)} all-to-all(bf16[16,1,32,512]{3,2,1,0:T(8,128)(2,1)S(1)} %divide_convert_fusion), channel_id=1, replica_groups=mesh['domain'=2,'fsdp'=16] {'fsdp'}, dimensions={0} | all-to-all | bytes 1048576 | tf_op jit(solution)/shard_map/all_to_all | solution.py:104
  78.0 2.5 collective-permute-done
  80.7 1.1 collective-permute-start.1
  81.8 24.2 %collective-permute-done.1 = f32[512,512]{1,0:T(8,128)S(1)} collective-permute-done((f32[512,512]{1,0:T(8,128)S(1)}, f32[512,512]{1,0:T(8,128)S(1)}, u32[]{:S(2)}, u32[]{:S(2)}) %collective-permute-start.1) | collective-permute-done | bytes 1048608 | tf_op jit(solution)/shard_map/ppermute | solution.py:22
  106.2 1.8 collective-permute-start.2
  108.0 22.8 %collective-permute-done.2 = f32[512,512]{1,0:T(8,128)S(1)} collective-permute-done((f32[512,512]{1,0:T(8,128)S(1)}, f32[512,512]{1,0:T(8,128)S(1)}, u32[]{:S(2)}, u32[]{:S(2)}) %collective-permute-start.2) | collective-permute-done | bytes 1048608 | tf_op jit(solution)/shard_map/ppermute | solution.py:22
  131.1 0.8 fusion.6
  132.4 2.6 %collective-permute-done.3 = f32[512,512]{1,0:T(8,128)S(1)} collective-permute-done((f32[512,512]{1,0:T(8,128)S(1)}, f32[512,512]{1,0:T(8,128)S(1)}, u32[]{:S(2)}, u32[]{:S(2)}) %collective-permute-start.3) | collective-permute-done | bytes 1048608 | tf_op jit(solution)/shard_map/ppermute | solution.py:22
  135.3 1.3 collective-permute-start.4
  136.6 23.9 %collective-permute-done.4 = f32[512,512]{1,0:T(8,128)S(1)} collective-permute-done((f32[512,512]{1,0:T(8,128)S(1)}, f32[512,512]{1,0:T(8,128)S(1)}, u32[]{:S(2)}, u32[]{:S(2)}) %collective-permute-start.4) | collective-permute-done | bytes 1048608 | tf_op jit(solution)/shard_map/ppermute | solution.py:22
  160.8 1.8 collective-permute-start.5
  162.6 22.6 %collective-permute-done.5 = f32[512,512]{1,0:T(8,128)S(1)} collective-permute-done((f32[512,512]{1,0:T(8,128)S(1)}, f32[512,512]{1,0:T(8,128)S(1)}, u32[]{:S(2)}, u32[]{:S(2)}) %collective-permute-start.5) | collective-permute-done | bytes 1048608 | tf_op jit(solution)/shard_map/ppermute | solution.py:22
  185.4 0.8 fusion.7
  186.8 2.6 %collective-permute-done.6 = f32[512,512]{1,0:T(8,128)S(1)} collective-permute-done((f32[512,512]{1,0:T(8,128)S(1)}, f32[512,512]{1,0:T(8,128)S(1)}, u32[]{:S(2)}, u32[]{:S(2)}) %collective-permute-start.6) | collective-permute-done | bytes 1048608 | tf_op jit(solution)/shard_map/ppermute | solution.py:22
  189.6 1.3 collective-permute-start.7
  190.9 24.0 %collective-permute-done.7 = f32[512,512]{1,0:T(8,128)S(1)} collective-permute-done((f32[512,512]{1,0:T(8,128)S(1)}, f32[512,512]{1,0:T(8,128)S(1)}, u32[]{:S(2)}, u32[]{:S(2)}) %collective-permute-start.7) | collective-permute-done | bytes 1048608 | tf_op jit(solution)/shard_map/ppermute | solution.py:22
  215.1 1.8 collective-permute-start.8
  216.9 22.6 %collective-permute-done.8 = f32[512,512]{1,0:T(8,128)S(1)} collective-permute-done((f32[512,512]{1,0:T(8,128)S(1)}, f32[512,512]{1,0:T(8,128)S(1)}, u32[]{:S(2)}, u32[]{:S(2)}) %collective-permute-start.8) | collective-permute-done | bytes 1048608 | tf_op jit(solution)/shard_map/ppermute | solution.py:22
  239.8 1.6 fusion.8
  241.3 4.3 %all-to-all-start.2 = ((bf16[1,16,32,512]{3,2,0,1:T(8,128)(2,1)}), bf16[1,16,32,512]{3,2,0,1:T(8,128)(2,1)S(1)}, u32[]{:S(2)}, u32[]{:S(2)}) async-start(bf16[1,16,32,512]{3,2,0,1:T(8,128)(2,1)} %bitcast.5), calls=%async_computation.2 | async-start | bytes 1048576 | tf_op jit(solution)/shard_map/all_to_all | solution.py:107
  245.8 1.3 fusion.21
  247.1 1.2 broadcast_divide_fusion
  248.3 11.6 %all-to-all-done.2 = bf16[1,16,32,512]{3,2,0,1:T(8,128)(2,1)S(1)} async-done(((bf16[1,16,32,512]{3,2,0,1:T(8,128)(2,1)}), bf16[1,16,32,512]{3,2,0,1:T(8,128)(2,1)S(1)}, u32[]{:S(2)}, u32[]{:S(2)}) %all-to-all-start.2) | async-done | bytes 524320 | tf_op jit(solution)/shard_map/all_to_all | solution.py:107
  260.0 1.1 convert_multiply_fusion
  (35 shorter events, 5.4 us)
Async XLA Ops:
  0.6 4.4 %copy-start.2 = (s32[2]{0:T(128)S(1)}, s32[2]{0:T(128)}, u32[]{:S(2)}) copy-start(s32[2]{0:T(128)} %param.6) | copy-start | bytes 28
  0.6 4.5 %copy-start = (f32[8]{0:T(128)S(1)}, f32[8]{0:T(128)}, u32[]{:S(2)}) copy-start(f32[8]{0:T(128)} %param.7) | copy-start | bytes 100
  0.7 5.1 %copy-start.1 = (s32[4]{0:T(128)S(1)}, s32[4]{0:T(128)}, u32[]{:S(2)}) copy-start(s32[4]{0:T(128)} %param.5) | copy-start | bytes 52
  0.7 18.8 %all-to-all-start = ((bf16[1,2,2,256,512]{4,3,2,0,1:T(8,128)(2,1)}), bf16[1,2,2,256,512]{4,3,2,0,1:T(8,128)(2,1)S(1)}, u32[]{:S(2)}, u32[]{:S(2)}) async-start(bf16[1,2,2,256,512]{4,3,2,0,1:T(8,128)(2,1)} %bitcast.31), calls=%async_computation | async-start | bytes 2097152 | tf_op jit(solution)/shard_map/all_to_all | solution.py:78
  77.8 2.7 %collective-permute-start = (f32[512,512]{1,0:T(8,128)S(1)}, f32[512,512]{1,0:T(8,128)S(1)}, u32[]{:S(2)}, u32[]{:S(2)}) collective-permute-start(f32[512,512]{1,0:T(8,128)S(1)} %fusion.22), channel_id=1, source_target_pairs={{0,1},{1,0},{2,3},{3,2},{4,5},{5,4},{6,7},{7,6},{8,9},{9,8},{10,11... | collective-permute-start | bytes 3145736 | tf_op jit(solution)/shard_map/ppermute | solution.py:22
  80.7 25.3 %collective-permute-start.1 = (f32[512,512]{1,0:T(8,128)S(1)}, f32[512,512]{1,0:T(8,128)S(1)}, u32[]{:S(2)}, u32[]{:S(2)}) collective-permute-start(f32[512,512]{1,0:T(8,128)S(1)} %add.82), channel_id=1, source_target_pairs={{0,2},{1,3},{2,0},{3,1},{4,6},{5,7},{6,4},{7,5},{8,10},{9,11},{10,... | collective-permute-start | bytes 3145736 | tf_op jit(solution)/shard_map/ppermute | solution.py:22
  106.2 24.6 %collective-permute-start.2 = (f32[512,512]{1,0:T(8,128)S(1)}, f32[512,512]{1,0:T(8,128)S(1)}, u32[]{:S(2)}, u32[]{:S(2)}) collective-permute-start(f32[512,512]{1,0:T(8,128)S(1)} %add.83), channel_id=1, source_target_pairs={{0,4},{1,5},{2,6},{3,7},{4,0},{5,1},{6,2},{7,3},{8,12},{9,13},{10,... | collective-permute-start | bytes 3145736 | tf_op jit(solution)/shard_map/ppermute | solution.py:22
  132.3 2.7 %collective-permute-start.3 = (f32[512,512]{1,0:T(8,128)S(1)}, f32[512,512]{1,0:T(8,128)S(1)}, u32[]{:S(2)}, u32[]{:S(2)}) collective-permute-start(f32[512,512]{1,0:T(8,128)S(1)} %fusion.23), channel_id=1, source_target_pairs={{0,1},{1,0},{2,3},{3,2},{4,5},{5,4},{6,7},{7,6},{8,9},{9,8},{10,11... | collective-permute-start | bytes 3145736 | tf_op jit(solution)/shard_map/ppermute | solution.py:22
  135.3 25.3 %collective-permute-start.4 = (f32[512,512]{1,0:T(8,128)S(1)}, f32[512,512]{1,0:T(8,128)S(1)}, u32[]{:S(2)}, u32[]{:S(2)}) collective-permute-start(f32[512,512]{1,0:T(8,128)S(1)} %add.87), channel_id=1, source_target_pairs={{0,2},{1,3},{2,0},{3,1},{4,6},{5,7},{6,4},{7,5},{8,10},{9,11},{10,... | collective-permute-start | bytes 3145736 | tf_op jit(solution)/shard_map/ppermute | solution.py:22
  160.8 24.4 %collective-permute-start.5 = (f32[512,512]{1,0:T(8,128)S(1)}, f32[512,512]{1,0:T(8,128)S(1)}, u32[]{:S(2)}, u32[]{:S(2)}) collective-permute-start(f32[512,512]{1,0:T(8,128)S(1)} %add.88), channel_id=1, source_target_pairs={{0,4},{1,5},{2,6},{3,7},{4,0},{5,1},{6,2},{7,3},{8,12},{9,13},{10,... | collective-permute-start | bytes 3145736 | tf_op jit(solution)/shard_map/ppermute | solution.py:22
  186.7 2.7 %collective-permute-start.6 = (f32[512,512]{1,0:T(8,128)S(1)}, f32[512,512]{1,0:T(8,128)S(1)}, u32[]{:S(2)}, u32[]{:S(2)}) collective-permute-start(f32[512,512]{1,0:T(8,128)S(1)} %fusion.24), channel_id=1, source_target_pairs={{0,1},{1,0},{2,3},{3,2},{4,5},{5,4},{6,7},{7,6},{8,9},{9,8},{10,11... | collective-permute-start | bytes 3145736 | tf_op jit(solution)/shard_map/ppermute | solution.py:22
  189.6 25.3 %collective-permute-start.7 = (f32[512,512]{1,0:T(8,128)S(1)}, f32[512,512]{1,0:T(8,128)S(1)}, u32[]{:S(2)}, u32[]{:S(2)}) collective-permute-start(f32[512,512]{1,0:T(8,128)S(1)} %add.92), channel_id=1, source_target_pairs={{0,2},{1,3},{2,0},{3,1},{4,6},{5,7},{6,4},{7,5},{8,10},{9,11},{10,... | collective-permute-start | bytes 3145736 | tf_op jit(solution)/shard_map/ppermute | solution.py:22
  215.1 24.4 %collective-permute-start.8 = (f32[512,512]{1,0:T(8,128)S(1)}, f32[512,512]{1,0:T(8,128)S(1)}, u32[]{:S(2)}, u32[]{:S(2)}) collective-permute-start(f32[512,512]{1,0:T(8,128)S(1)} %add.93), channel_id=1, source_target_pairs={{0,4},{1,5},{2,6},{3,7},{4,0},{5,1},{6,2},{7,3},{8,12},{9,13},{10,... | collective-permute-start | bytes 3145736 | tf_op jit(solution)/shard_map/ppermute | solution.py:22
  241.3 18.6 %all-to-all-start.2 = ((bf16[1,16,32,512]{3,2,0,1:T(8,128)(2,1)}), bf16[1,16,32,512]{3,2,0,1:T(8,128)(2,1)S(1)}, u32[]{:S(2)}, u32[]{:S(2)}) async-start(bf16[1,16,32,512]{3,2,0,1:T(8,128)(2,1)} %bitcast.5), calls=%async_computation.2 | async-start | bytes 1048576 | tf_op jit(solution)/shard_map/all_to_all | solution.py:107
